TPU v7x, 32 devices: a whole 2x2x4 slice. The times are simulated.
32 devices in a mesh: groups: 2 (over x), paths: 2 (over core), feats: 8 (over z, y).
Axes of the slice: x: 2, y: 2, z: 4, core: 2. Of those that a mesh axis runs over, the one named last changes fastest.
Arguments:
- factors: int32 [4096, 128], P(('groups', 'paths')), parts along dimension 0, may hold values from -8 to 8
- frequency: int32 [128, 65536], P(None, 'feats'), may hold values from -48 to 48
- phases: int32 [65536], P('feats'), may hold values from 0 to 1023
- amplitude: float32 [65536], P('feats'), as said below
- targets: float32 [32, 4096], P(None, ('groups', 'paths')), parts along dimension 1, may hold values from -6 to 6
- coeffs_init: float32 [32, 131072], P(None, ('groups', 'feats')), parts along dimension 1, may hold values from -6 to 6
Outputs:
- coeffs: float32 [32, 131072], P(None, ('groups', 'feats')), parts along dimension 1
- predicted: float32 [32, 4096], P(None, ('groups', 'paths')), parts along dimension 1
There are 2 independent parts, one for each index of `groups`. A program takes and returns all parts, laid end to end along the dimension named above; an argument that names none is the same for every part. Nothing has to cross between parts.
Inputs may be any that keep to these rules, and one draw needn't show every extreme that they name: `amplitude`: positive feature weights.
All inputs are finite; a program needn't handle non-finite values.
Results may differ from a plain program's by a relative error of at most 0.00026.
Values sent between devices are 32-bit elements; how exact they have to be, the bound alone decides.
A program may use at most 128 MiB of HBM per device.

v0:
```python
import math

import jax
import jax.numpy as jnp
from jax import lax
from jax.sharding import PartitionSpec as P

F = 65536
V = 32
ITERS = 3


huber_cap = 1.0
step_rate = 0.2
momentum = 0.9
epsilon = 1e-06


def build(factor_vals, freq_block, phase_block, amp_block):
    summed = jnp.dot(
        factor_vals, freq_block, precision=lax.Precision.HIGHEST, preferred_element_type=jnp.float32
    )
    return amp_block * jnp.cos(summed * 0.0025 + phase_block * (2.0 * math.pi / 1024.0))


def image_of(coeffs, block):
    return lax.dot_general(
        coeffs,
        block,
        (((1,), (1,)), ((), ())),
        precision=lax.Precision.HIGHEST,
        preferred_element_type=jnp.float32,
    )


def shards(factors, frequency, phases, amplitude, targets, coeffs_init):
    factor_vals = factors.astype(jnp.float32)
    freq_vals = frequency.astype(jnp.float32)
    phase_vals = phases.astype(jnp.float32)
    stored = build(factor_vals, freq_vals, phase_vals, amplitude)

    def features_now():
        return stored

    coeffs = coeffs_init
    velocity = jnp.zeros_like(coeffs_init)
    tracked = jnp.zeros_like(targets)
    predicted = lax.psum(image_of(coeffs, features_now()), "feats")
    for turn in range(ITERS):
        block = features_now()
        clipped = jnp.clip(predicted - targets, -huber_cap, huber_cap)
        local_grad = jnp.dot(
            clipped, block, precision=lax.Precision.HIGHEST, preferred_element_type=jnp.float32
        )
        gradient = lax.psum(local_grad, "paths")
        pushed, squares = lax.psum(
            (image_of(gradient, block), jnp.sum(gradient * gradient)), "feats"
        )
        scale = jnp.sqrt(squares / (V * F) + epsilon)
        velocity = momentum * velocity + gradient / scale
        coeffs = coeffs - step_rate * velocity
        tracked = momentum * tracked + pushed / scale
        predicted = predicted - step_rate * tracked
    return (coeffs, predicted)


def solution(mesh):
    return jax.shard_map(
        shards,
        mesh=mesh,
        in_specs=(
            P(("groups", "paths"), None),
            P(None, "feats"),
            P("feats"),
            P("feats"),
            P(None, ("groups", "paths")),
            P(None, ("groups", "feats")),
        ),
        out_specs=(P(None, ("groups", "feats")), P(None, ("groups", "paths"))),
        check_vma=False,
    )
```

profile of v0, /device:TPU:0, one launch (start us, length us, event | category | flops | bytes accessed | tf_op | source)
XLA Modules:
  0.0 752.4 jit_solution(18103428148732155704)
XLA Ops:
  7.2 0.0 all-reduce.8.cloned.1.call-start
  7.2 0.8 convert_multiply_fusion
  8.1 139.3 %cosine_multiply_fusion = f32[1024,8192]{1,0:T(8,128)} fusion(f32[8192]{0:T(1024)S(1)} %convert_multiply_fusion, f32[8192]{0:T(1024)} %param.9, s32[128,8192]{1,0:T(8,128)} %param.7, s32[1024,128]{1,0:T(8,128)} %param.6), kind=kOutput, calls=%fused_computation | convolution fusion | flops 12911247360 | bytes 38338560 | tf_op jit(solution)/shard_map/dot_general | solution.py:20
  147.4 34.8 %convolution_bitcast_fusion = f32[32,1024]{1,0:T(8,128)} fusion(f32[1024,8192]{1,0:T(8,128)} %cosine_multiply_fusion, f32[32,8192]{1,0:T(8,128)S(1)} %copy-done.3), kind=kOutput, calls=%fused_computation.2 | convolution fusion | flops 3221225472 | bytes 34734080 | tf_op jit(solution)/shard_map/dot_general | solution.py:27
  182.2 0.2 all-reduce.10.cloned.1.call-start
  182.4 73.0 %all-reduce.8.cloned.1.call-done = f32[32,1024]{1,0:T(8,128)} async-done(((f32[32,1024]{1,0:T(8,128)}), f32[32,1024]{1,0:T(8,128)}) %all-reduce.8.cloned.1.call-update) | async-done | bytes 131088 | tf_op jit(solution)/shard_map/psum | solution.py:48
  255.5 30.2 %fusion.8 = f32[32,8192]{1,0:T(8,128)} fusion(f32[1024,8192]{1,0:T(8,128)} %cosine_multiply_fusion, f32[32,1024]{1,0:T(8,128)} %all-reduce.8.cloned.1.call-done, f32[32,1024]{1,0:T(8,128)S(1)} %copy-done.4), kind=kOutput, calls=%fused_computation.18 | convolution fusion | flops 3221291008 | bytes 34865152 | tf_op jit(solution)/shard_map/dot_general | solution.py:52
  285.7 0.4 all-reduce.12.cloned.1.call-start
  286.2 18.2 %all-reduce.10.cloned.1.call-done = f32[32,8192]{1,0:T(8,128)} async-done(((f32[32,8192]{1,0:T(8,128)}), f32[32,8192]{1,0:T(8,128)}) %all-reduce.10.cloned.1.call-update) | async-done | bytes 1048592 | tf_op jit(solution)/shard_map/psum | solution.py:55
  304.4 36.7 %fusion.25 = f32[32,1024]{1,0:T(8,128)} fusion(f32[32,8192]{1,0:T(8,128)} %all-reduce.10.cloned.1.call-done, f32[1024,8192]{1,0:T(8,128)} %cosine_multiply_fusion), kind=kOutput, calls=%fused_computation.37 | convolution fusion | flops 3221225472 | bytes 34734080 | tf_op jit(solution)/shard_map/dot_general | solution.py:27
  341.1 0.0 all-reduce.14.cloned.1.call-start
  341.2 0.9 multiply_reduce_fusion.2
  342.1 22.5 %psum.72 = f32[]{:T(128)} all-reduce(f32[]{:T(128)} %multiply_reduce_fusion.2), channel_id=1, replica_groups=mesh['groups'=2,'paths'=2,'feats'=8] {'feats'}, use_global_device_ids=true, to_apply=%region_3.4 | all-reduce | flops 1 | bytes 8 | tf_op jit(solution)/shard_map/psum | solution.py:56
  365.2 47.7 %all-reduce.12.cloned.1.call-done = f32[32,1024]{1,0:T(8,128)} async-done(((f32[32,1024]{1,0:T(8,128)}), f32[32,1024]{1,0:T(8,128)}) %all-reduce.12.cloned.1.call-update) | async-done | bytes 131088 | tf_op jit(solution)/shard_map/psum | solution.py:56
  412.9 0.9 multiply_subtract_fusion.3
  413.9 23.8 %fusion.5 = f32[32,8192]{1,0:T(8,128)} fusion(f32[1024,8192]{1,0:T(8,128)} %cosine_multiply_fusion, f32[32,1024]{1,0:T(8,128)S(1)} %multiply_subtract_fusion.3, f32[32,1024]{1,0:T(8,128)S(1)} %copy-done.4), kind=kOutput, calls=%fused_computation.14 | convolution fusion | flops 3221291008 | bytes 34865152 | tf_op jit(solution)/shard_map/dot_general | solution.py:52
  437.7 0.0 all-reduce.16.cloned.1.call-start
  437.8 18.6 %all-reduce.14.cloned.1.call-done = f32[32,8192]{1,0:T(8,128)} async-done(((f32[32,8192]{1,0:T(8,128)}), f32[32,8192]{1,0:T(8,128)}) %all-reduce.14.cloned.1.call-update) | async-done | bytes 1048592 | tf_op jit(solution)/shard_map/psum | solution.py:55
  456.4 36.7 %fusion.26 = f32[32,1024]{1,0:T(8,128)} fusion(f32[32,8192]{1,0:T(8,128)} %all-reduce.14.cloned.1.call-done, f32[1024,8192]{1,0:T(8,128)} %cosine_multiply_fusion), kind=kOutput, calls=%fused_computation.38 | convolution fusion | flops 3221225472 | bytes 34734080 | tf_op jit(solution)/shard_map/dot_general | solution.py:27
  493.1 0.0 all-reduce.18.cloned.1.call-start
  493.2 0.9 multiply_reduce_fusion.1
  494.1 22.7 %psum.75 = f32[]{:T(128)} all-reduce(f32[]{:T(128)} %multiply_reduce_fusion.1), channel_id=1, replica_groups=mesh['groups'=2,'paths'=2,'feats'=8] {'feats'}, use_global_device_ids=true, to_apply=%region_7.8 | all-reduce | flops 1 | bytes 8 | tf_op jit(solution)/shard_map/psum | solution.py:56
  517.4 47.5 %all-reduce.16.cloned.1.call-done = f32[32,1024]{1,0:T(8,128)} async-done(((f32[32,1024]{1,0:T(8,128)}), f32[32,1024]{1,0:T(8,128)}) %all-reduce.16.cloned.1.call-update) | async-done | bytes 131088 | tf_op jit(solution)/shard_map/psum | solution.py:56
  564.9 30.3 %fusion.2 = f32[32,8192]{1,0:T(8,128)} fusion(f32[1024,8192]{1,0:T(8,128)} %cosine_multiply_fusion, f32[32,1024]{1,0:T(8,128)S(1)} %copy-done.4, f32[32,1024]{1,0:T(8,128)S(1)} %multiply_subtract_fusion.3, f32[32,1024]{1,0:T(8,128)} %all-reduce.16.cloned.1.call-done, f32[]{:T(128)S(6)} %sqrt.10, f32[32,1024]{1,0:T(8,128)S(1)} %copy-done.5, f32[]{:T(128)S(6)} %sqrt.9), kind=kOutput, calls=%fused_computation.9 | convolution fusion | flops 3221487616 | bytes 35127304 | tf_op jit(solution)/shard_map/dot_general | solution.py:52
  595.2 0.0 all-reduce.20.cloned.1.call-start
  595.3 18.6 %all-reduce.18.cloned.1.call-done = f32[32,8192]{1,0:T(8,128)} async-done(((f32[32,8192]{1,0:T(8,128)}), f32[32,8192]{1,0:T(8,128)}) %all-reduce.18.cloned.1.call-update) | async-done | bytes 1048592 | tf_op jit(solution)/shard_map/psum | solution.py:55
  613.9 2.2 multiply_reduce_fusion
  616.1 22.4 %psum.78 = f32[]{:T(128)} all-reduce(f32[]{:T(128)} %multiply_reduce_fusion), channel_id=1, replica_groups=mesh['groups'=2,'paths'=2,'feats'=8] {'feats'}, use_global_device_ids=true, to_apply=%region_11.12 | all-reduce | flops 1 | bytes 8 | tf_op jit(solution)/shard_map/psum | solution.py:56
  639.2 36.7 %fusion.27 = f32[32,1024]{1,0:T(8,128)} fusion(f32[32,8192]{1,0:T(8,128)} %all-reduce.18.cloned.1.call-done, f32[1024,8192]{1,0:T(8,128)} %cosine_multiply_fusion), kind=kOutput, calls=%fused_computation.39 | convolution fusion | flops 3221225472 | bytes 34734080 | tf_op jit(solution)/shard_map/dot_general | solution.py:27
  675.9 2.6 multiply_subtract_fusion
  678.6 65.1 %all-reduce.20.cloned.1.call-done = f32[32,1024]{1,0:T(8,128)} async-done(((f32[32,1024]{1,0:T(8,128)}), f32[32,1024]{1,0:T(8,128)}) %all-reduce.20.cloned.1.call-update) | async-done | bytes 131088 | tf_op jit(solution)/shard_map/psum | solution.py:56
  743.7 1.6 multiply_subtract_fusion.1
  (23 shorter events, 0.1 us)
Async XLA Ops:
  7.2 140.2 %copy-start.3 = (f32[32,8192]{1,0:T(8,128)S(1)}, f32[32,8192]{1,0:T(8,128)}, u32[]{:S(2)}) copy-start(f32[32,8192]{1,0:T(8,128)} %param.11) | copy-start | bytes 3145732
  7.2 248.3 %all-reduce.8.cloned.1.call-start = ((), (), s32[]{:S(2)}) async-start(), calls=%async_computation | async-start | bytes 262144 | tf_op jit(solution)/shard_map/psum | solution.py:48
  8.1 247.4 %copy-start.4 = (f32[32,1024]{1,0:T(8,128)S(1)}, f32[32,1024]{1,0:T(8,128)}, u32[]{:S(2)}) copy-start(f32[32,1024]{1,0:T(8,128)} %param.10) | copy-start | bytes 393220
  182.2 122.2 %all-reduce.10.cloned.1.call-start = ((), (), s32[]{:S(2)}) async-start(), calls=%async_computation.1 | async-start | bytes 2097152 | tf_op jit(solution)/shard_map/psum | solution.py:55
  255.5 157.4 %copy-start.6 = (f32[32,1024]{1,0:T(8,128)S(1)}, f32[32,1024]{1,0:T(8,128)}, u32[]{:S(2)}) copy-start(f32[32,1024]{1,0:T(8,128)} %all-reduce.8.cloned.1.call-done) | copy-start | bytes 393220
  285.7 127.2 %all-reduce.12.cloned.1.call-start = ((), (), s32[]{:S(2)}) async-start(), calls=%async_computation.2 | async-start | bytes 262144 | tf_op jit(solution)/shard_map/psum | solution.py:56
  304.4 36.8 %copy-start = (f32[32,8192]{1,0:T(8,128)S(1)}, f32[32,8192]{1,0:T(8,128)}, u32[]{:S(2)}) copy-start(f32[32,8192]{1,0:T(8,128)} %all-reduce.10.cloned.1.call-done) | copy-start | bytes 3145732
  341.1 115.3 %all-reduce.14.cloned.1.call-start = ((), (), s32[]{:S(2)}) async-start(), calls=%async_computation.3 | async-start | bytes 2097152 | tf_op jit(solution)/shard_map/psum | solution.py:55
  413.9 151.1 %copy-start.5 = (f32[32,1024]{1,0:T(8,128)S(1)}, f32[32,1024]{1,0:T(8,128)}, u32[]{:S(2)}) copy-start(f32[32,1024]{1,0:T(8,128)} %all-reduce.12.cloned.1.call-done) | copy-start | bytes 393220
  437.7 127.2 %all-reduce.16.cloned.1.call-start = ((), (), s32[]{:S(2)}) async-start(), calls=%async_computation.4 | async-start | bytes 262144 | tf_op jit(solution)/shard_map/psum | solution.py:56
  456.4 36.8 %copy-start.1 = (f32[32,8192]{1,0:T(8,128)S(1)}, f32[32,8192]{1,0:T(8,128)}, u32[]{:S(2)}) copy-start(f32[32,8192]{1,0:T(8,128)} %all-reduce.14.cloned.1.call-done) | copy-start | bytes 3145732
  493.1 120.8 %all-reduce.18.cloned.1.call-start = ((), (), s32[]{:S(2)}) async-start(), calls=%async_computation.5 | async-start | bytes 2097152 | tf_op jit(solution)/shard_map/psum | solution.py:55
  564.9 178.8 %copy-start.7 = (f32[32,1024]{1,0:T(8,128)S(1)}, f32[32,1024]{1,0:T(8,128)}, u32[]{:S(2)}) copy-start(f32[32,1024]{1,0:T(8,128)} %all-reduce.16.cloned.1.call-done) | copy-start | bytes 393220
  595.2 148.5 %all-reduce.20.cloned.1.call-start = ((), (), s32[]{:S(2)}) async-start(), calls=%async_computation.6 | async-start | bytes 262144 | tf_op jit(solution)/shard_map/psum | solution.py:56
  613.9 62.0 %copy-start.2 = (f32[32,8192]{1,0:T(8,128)S(1)}, f32[32,8192]{1,0:T(8,128)}, u32[]{:S(2)}) copy-start(f32[32,8192]{1,0:T(8,128)} %all-reduce.18.cloned.1.call-done) | copy-start | bytes 3145732
Sparse Core Ops, SparseCore 0:
  182.3 73.1 all-reduce.7
  285.8 18.5 all-reduce.9
  341.3 71.6 all-reduce.11
  437.9 18.4 all-reduce.13
  493.3 71.6 all-reduce.15
  595.3 18.5 all-reduce.17
  676.0 67.6 all-reduce.19
where the time goes:
time: 760 us; the launch traced here: 752 us
  matrix products  369 us (49%)
  waiting for transfers between devices  289 us (38%)
  blocking collectives  67.6 us (9%)
  between operations  16.5 us (2%)
  other arithmetic  9.95 us (1%)
    psum x3, waiting for transfers between devices, shards(): lax.psum((image_of(gradient, block), jnp.sum(gradient * gradient)), 'feats')  160 us
    dot_general x4, matrix products, image_of(): lax.dot_general(coeffs, block, (((1,), (1,)), ((), ())), precision=lax.Pr...  145 us
    dot_general x1, matrix products, build(): jnp.dot(factor_vals, freq_block, precision=lax.Precision.HIGHEST, preferr...  139 us
    dot_general x3, matrix products, shards(): jnp.dot(clipped, block, precision=lax.Precision.HIGHEST, preferred_elemen...  84.3 us
    psum x1, waiting for transfers between devices, shards(): predicted = lax.psum(image_of(coeffs, features_now()), 'feats')  73 us
    psum x3, blocking collectives, shards(): lax.psum((image_of(gradient, block), jnp.sum(gradient * gradient)), 'feats')  67.6 us
    psum x3, waiting for transfers between devices, shards(): gradient = lax.psum(local_grad, 'paths')  55.5 us
  transfers between devices with their start and end apart: 7, of which 7 were waited for; matrix products, arithmetic and copies ran while one was open for 1% of the time, Pallas kernels for 0%

commit v1 on v0

v1 whole, which is shorter than its diff:
```python
import functools
import math

import jax
import jax.numpy as jnp
import numpy as np
from jax import lax
from jax.experimental import pallas as pl
from jax.experimental.pallas import tpu as pltpu
from jax.sharding import PartitionSpec as P

huber_cap = 1.0
step_rate = 0.2
momentum = 0.9
epsilon = 1e-06
ITERS = 3
BF = jnp.bfloat16
F32 = jnp.float32


def cosine_fit(degree):
    n = 64
    nodes = np.cos((np.arange(n) + 0.5) * np.pi / n)
    u = (nodes + 1.0) / 8.0
    cheb = np.polynomial.chebyshev.Chebyshev.fit(u, np.cos(2 * np.pi * np.sqrt(u)), degree, domain=[0.0, 0.25])
    return [float(c) for c in cheb.convert(kind=np.polynomial.Polynomial).coef]


COEFS = cosine_fit(5)
TURN = 0.0025 / (2.0 * math.pi)
MAGIC = 12582912.0


def cos_turns(t):
    k = (t + MAGIC) - MAGIC
    r = t - k
    u = r * r
    acc = u * COEFS[-1] + COEFS[-2]
    for c in COEFS[-3::-1]:
        acc = acc * u + c
    return acc


def split(x):
    hi = x.astype(BF)
    lo = (x - hi.astype(F32)).astype(BF)
    return hi, lo


def stacked(x):
    hi, lo = split(x)
    return jnp.concatenate([hi, lo], axis=0)


NT = (((1,), (1,)), ((), ()))


def build_kernel(half_ref, fac_ref, freq_ref, phase_ref, amp_ref, coef_ref, hi_ref, lo_ref, pred_ref, *, rows):
    @pl.when(pl.program_id(0) == 0)
    def _():
        pred_ref[...] = jnp.zeros_like(pred_ref)

    freq = freq_ref[...].astype(F32).astype(BF)
    phase = phase_ref[...].astype(F32) * (1.0 / 1024.0)
    chunks = fac_ref.shape[0] // rows

    def step(i, carry):
        at = pl.ds(pl.multiple_of(i * rows, rows), rows)
        summed = jnp.dot(fac_ref[at, :], freq, preferred_element_type=F32)
        c = cos_turns(summed * TURN + phase)
        hi, lo = split(c)
        hi_ref[at, :] = hi
        lo_ref[at, :] = lo
        return carry

    lax.fori_loop(0, chunks, step, 0, unroll=2)
    v = coef_ref.shape[0]
    x = stacked(coef_ref[...] * amp_ref[...])
    out = lax.dot_general(x, hi_ref[...], NT, preferred_element_type=F32)
    out = out + lax.dot_general(x, lo_ref[...], NT, preferred_element_type=F32)
    pred_ref[...] += out[:v] + out[v:]


def build(half, factors, frequency, phases, amplitude, coeffs, tile):
    paths, k = factors.shape
    v, whole = coeffs.shape
    mine = whole // 2
    nb = mine // tile
    at = lambda i, h: (0, h[0] * nb + i)
    return pl.pallas_call(
        functools.partial(build_kernel, rows=128),
        grid_spec=pltpu.PrefetchScalarGridSpec(
            num_scalar_prefetch=1,
            grid=(nb,),
            in_specs=[
                pl.BlockSpec((paths, k), lambda i, h: (0, 0)),
                pl.BlockSpec((k, tile), at),
                pl.BlockSpec((1, tile), at),
                pl.BlockSpec((1, tile), at),
                pl.BlockSpec((v, tile), at),
            ],
            out_specs=[
                pl.BlockSpec((paths, tile), lambda i, h: (0, i)),
                pl.BlockSpec((paths, tile), lambda i, h: (0, i)),
                pl.BlockSpec((v, paths), lambda i, h: (0, 0)),
            ],
        ),
        out_shape=[
            jax.ShapeDtypeStruct((paths, mine), BF),
            jax.ShapeDtypeStruct((paths, mine), BF),
            jax.ShapeDtypeStruct((v, paths), F32),
        ],
        name="build",
    )(half, factors, frequency, phases, amplitude, coeffs)


def turn_kernel(half_ref, clip_ref, amp_ref, hi_ref, lo_ref, grad_ref, push_ref, sq_ref, clip_pair):
    @pl.when(pl.program_id(0) == 0)
    def _():
        push_ref[...] = jnp.zeros_like(push_ref)
        sq_ref[...] = jnp.zeros_like(sq_ref)
        clip_pair[...] = stacked(clip_ref[...])

    v = grad_ref.shape[0]
    x = clip_pair[...]
    g = jnp.dot(x, hi_ref[...], preferred_element_type=F32)
    g = g + jnp.dot(x, lo_ref[...], preferred_element_type=F32)
    amp = amp_ref[...]
    grad = (g[:v] + g[v:]) * amp
    grad_ref[...] = grad
    square = grad * grad
    fold = sum(square[r : r + 8] for r in range(0, v, 8))
    sq_ref[...] += sum(fold[:, c : c + 128] for c in range(0, fold.shape[1], 128))
    y = stacked(grad * amp)
    out = lax.dot_general(y, hi_ref[...], NT, preferred_element_type=F32)
    out = out + lax.dot_general(y, lo_ref[...], NT, preferred_element_type=F32)
    push_ref[...] += out[:v] + out[v:]


def turn(half, clipped, amplitude, hi, lo, tile):
    v, paths = clipped.shape
    mine = hi.shape[1]
    nb = mine // tile
    return pl.pallas_call(
        turn_kernel,
        grid_spec=pltpu.PrefetchScalarGridSpec(
            num_scalar_prefetch=1,
            grid=(nb,),
            in_specs=[
                pl.BlockSpec((v, paths), lambda i, h: (0, 0)),
                pl.BlockSpec((1, tile), lambda i, h: (0, h[0] * nb + i)),
                pl.BlockSpec((paths, tile), lambda i, h: (0, i)),
                pl.BlockSpec((paths, tile), lambda i, h: (0, i)),
            ],
            out_specs=[
                pl.BlockSpec((v, tile), lambda i, h: (0, i)),
                pl.BlockSpec((v, paths), lambda i, h: (0, 0)),
                pl.BlockSpec((8, 128), lambda i, h: (0, 0)),
            ],
            scratch_shapes=[pltpu.VMEM((2 * v, paths), BF)],
        ),
        out_shape=[
            jax.ShapeDtypeStruct((v, mine), F32),
            jax.ShapeDtypeStruct((v, paths), F32),
            jax.ShapeDtypeStruct((8, 128), F32),
        ],
        name="turn",
    )(half, clipped, amplitude, hi, lo)


MESH = pl.DeviceIdType.MESH


def sum_kernel(x_ref, sq_ref, out_ref, sqout_ref, from_pair, chip, pieces, result, sq_pair, sq_mine, sq_all, total,
               pair_send, pair_recv, rs_send, rs_recv, ag_send, ag_recv, back_send, back_recv, sqp_sem, sqs_send, sqs_recv,
               *, n, rows, width, per_row):
    v, half_cols = chip.shape
    core = lax.axis_index("paths")
    me = lax.axis_index("feats")
    other = 1 - core

    barrier = pltpu.get_barrier_semaphore()
    pl.semaphore_signal(barrier, inc=1, device_id={"paths": other}, device_id_type=MESH)
    for d in range(1, n):
        pl.semaphore_signal(barrier, inc=1, device_id={"feats": lax.rem(me + d, n)}, device_id_type=MESH)
    pl.semaphore_wait(barrier, n)

    def spot(j, base):
        r = pl.ds(pl.multiple_of((j // per_row) * rows, rows), rows)
        c = pl.ds(pl.multiple_of(base + lax.rem(j, per_row) * width, width), width)
        return r, c

    def to_pair(src, dst, ss, rs):
        return pltpu.make_async_remote_copy(src, dst, ss, rs, device_id={"paths": other}, device_id_type=MESH)

    def to_chip(src, dst, ss, rs, j):
        return pltpu.make_async_remote_copy(src, dst, ss, rs, device_id={"feats": j}, device_id_type=MESH)

    zero = 0
    sq_copy = to_pair(sq_ref, sq_pair, sqp_sem.at[0], sqp_sem.at[1])
    sq_copy.start()
    pair_copies = []
    for d in range(1, n + 1):
        j = lax.rem(me + d, n)
        r, c = spot(j, other * half_cols)
        r2, c2 = spot(j, zero)
        pair_copies.append(to_pair(x_ref.at[r, c], from_pair.at[r2, c2], pair_send.at[d - 1], pair_recv.at[d - 1]))
        pair_copies[-1].start()

    sq_copy.wait()
    sq_mine[...] = sq_ref[...] + sq_pair[...]
    sq_all[me] = sq_mine[...]
    rs_copies, sq_copies = [], []
    for d in range(1, n + 1):
        j = lax.rem(me + d, n)
        pair_copies[d - 1].wait_recv()
        r, c = spot(j, core * half_cols)
        r2, c2 = spot(j, zero)
        chip[r2, c2] = x_ref[r, c] + from_pair[r2, c2]
        if d < n:
            rs_copies.append(to_chip(chip.at[r2, c2], pieces.at[d - 1], rs_send.at[d - 1], rs_recv.at[d - 1], j))
            rs_copies[-1].start()
    for d in range(1, n):
        j = lax.rem(me + d, n)
        sq_copies.append(to_chip(sq_mine, sq_all.at[me], sqs_send.at[d - 1], sqs_recv.at[d - 1], j))
        sq_copies[-1].start()

    mr, mc = spot(me, zero)
    acc = chip[mr, mc]
    for d in range(1, n):
        rs_copies[d - 1].wait_recv()
        acc = acc + pieces[d - 1]
    total[...] = acc

    br, bc = spot(me, core * half_cols)
    ag_copies, back_copies = [], []
    for d in range(1, n):
        j = lax.rem(me + d, n)
        ag_copies.append(to_chip(total, result.at[br, bc], ag_send.at[d - 1], ag_recv.at[d - 1], j))
        ag_copies[-1].start()
    back_copies.append(to_pair(total, result.at[br, bc], back_send.at[0], back_recv.at[0]))
    back_copies[0].start()
    result[br, bc] = acc
    for d in range(1, n):
        ag_copies[d - 1].wait_recv()
        source = lax.rem(me + n - d, n)
        r, c = spot(source, core * half_cols)
        back_copies.append(to_pair(result.at[r, c], result.at[r, c], back_send.at[d], back_recv.at[d]))
        back_copies[-1].start()
    for copy in sq_copies:
        copy.wait()
    sqout_ref[...] = jnp.broadcast_to(jnp.sum(jnp.sum(sq_all[...], axis=0), keepdims=True), sqout_ref.shape)
    for copy in pair_copies:
        copy.wait_send()
    for copy in rs_copies:
        copy.wait_send()
    for copy in ag_copies:
        copy.wait_send()
    for copy in back_copies:
        copy.wait()
    out_ref[...] = result[...]


def sum_over(partial, squares, n):
    v, cols = partial.shape
    half_cols = cols // 2
    per_row = min(n, half_cols // 128)
    width = half_cols // per_row
    rows = v // (n // per_row)
    dma = pltpu.SemaphoreType.DMA
    vm = pl.BlockSpec(memory_space=pltpu.VMEM)
    return pl.pallas_call(
        functools.partial(sum_kernel, n=n, rows=rows, width=width, per_row=per_row),
        in_specs=[vm, vm],
        out_specs=[vm, vm],
        out_shape=[jax.ShapeDtypeStruct((v, cols), F32), jax.ShapeDtypeStruct((8, 128), F32)],
        scratch_shapes=[
            pltpu.VMEM((v, half_cols), F32),
            pltpu.VMEM((v, half_cols), F32),
            pltpu.VMEM((n - 1, rows, width), F32),
            pltpu.VMEM((v, cols), F32),
            pltpu.VMEM((8, 128), F32),
            pltpu.VMEM((8, 128), F32),
            pltpu.VMEM((n, 8, 128), F32),
            pltpu.VMEM((rows, width), F32),
            dma((n,)), dma((n,)), dma((n - 1,)), dma((n - 1,)), dma((n - 1,)), dma((n - 1,)),
            dma((n,)), dma((n,)), dma((2,)), dma((n - 1,)), dma((n - 1,)),
        ],
        compiler_params=pltpu.CompilerParams(collective_id=0, has_side_effects=True),
        name="sum_over",
    )(partial, squares)


def from_both(x, half, axis):
    other = lax.ppermute(x, "paths", [(0, 1), (1, 0)])
    first = jnp.where(half == 0, x, other)
    second = jnp.where(half == 0, other, x)
    return jnp.concatenate([first, second], axis=axis)


def shards(total_features, chips, factors, frequency, phases, amplitude, targets, coeffs_init):
    half = lax.axis_index("paths")
    pick = half[None].astype(jnp.int32)
    v, block = coeffs_init.shape
    own_paths = targets.shape[1]
    mine = block // 2
    factors_all = from_both(factors, half, 0).astype(F32).astype(BF)
    targets_all = from_both(targets, half, 1)
    amp_row = amplitude[None, :]
    own_init = lax.dynamic_slice_in_dim(coeffs_init, half * mine, mine, 1)

    hi, lo, partial = build(pick, factors_all, frequency, phases[None, :], amp_row, coeffs_init, 256)
    predicted, _ = sum_over(partial, jnp.zeros((8, 128), F32), chips)
    coeffs = own_init
    velocity = jnp.zeros_like(own_init)
    tracked = jnp.zeros_like(predicted)
    for _ in range(ITERS):
        clipped = jnp.clip(predicted - targets_all, -huber_cap, huber_cap)
        gradient, push, squares = turn(pick, clipped, amp_row, hi, lo, 512)
        push, squares = sum_over(push, squares, chips)
        squares = squares[0, 0]
        scale = jnp.sqrt(squares / (v * total_features) + epsilon)
        velocity = momentum * velocity + gradient / scale
        coeffs = coeffs - step_rate * velocity
        tracked = momentum * tracked + push / scale
        predicted = predicted - step_rate * tracked
    coeffs = from_both(coeffs, half, 1)
    return coeffs, lax.dynamic_slice_in_dim(predicted, half * own_paths, own_paths, 1)


def solution(mesh):
    def body(factors, frequency, phases, amplitude, targets, coeffs_init):
        total = frequency.shape[1] * mesh.shape["feats"]
        return shards(total, mesh.shape["feats"], factors, frequency, phases, amplitude, targets, coeffs_init)

    return jax.shard_map(
        body,
        mesh=mesh,
        in_specs=(
            P(("groups", "paths"), None),
            P(None, "feats"),
            P("feats"),
            P("feats"),
            P(None, ("groups", "paths")),
            P(None, ("groups", "feats")),
        ),
        out_specs=(P(None, ("groups", "feats")), P(None, ("groups", "paths"))),
        check_vma=False,
    )
```

time: 760 us -> 213 us (0.28)
  matrix products: 369 us -> 0 us
  waiting for transfers between devices: 289 us -> 1.86 us
  Pallas kernels: 0 us -> 190 us
  blocking collectives: 67.6 us -> 0 us
  between operations: 16.5 us -> 2.82 us
    dot_general x8 -> x0, matrix products: 369 us -> none  [the longest x4 145 us: image_of(): lax.dot_general(coeffs, block, (((1,), (1,)), ((), ())), precision=lax.Pr...]
    psum x7 -> x0, waiting for transfers between devices: 289 us -> none  [the longest x3 160 us: shards(): lax.psum((image_of(gradient, block), jnp.sum(gradient * gradient)), 'feats')]
    pallas_call x0 -> x8, Pallas kernels: none -> 190 us  [the longest x4 69.7 us: sum_over(): pl.pallas_call(functools.partial(sum_kernel, n=n, rows=rows, width=width,...]
    psum x3 -> x0, blocking collectives: 67.6 us -> none  [shards(): lax.psum((image_of(gradient, block), jnp.sum(gradient * gradient)), 'feats')]
  transfers between devices with their start and end apart: 7 -> 3, of which waited for: 7 -> 1; matrix products, arithmetic and copies ran while one was open for 1% -> 1% of each run, Pallas kernels for 0% -> 0%
where the time goes in v1:
time: 213 us; the launch traced here: 212 us
  Pallas kernels  190 us (89%)
  other arithmetic  12 us (6%)
  local copies, waits for them, and re-layouts  4.18 us (2%)
  between operations  2.82 us (1%)
    pallas_call x4, Pallas kernels, sum_over(): pl.pallas_call(functools.partial(sum_kernel, n=n, rows=rows, width=width,...  69.7 us
    pallas_call x3, Pallas kernels, turn(): pl.pallas_call(turn_kernel, grid_spec=pltpu.PrefetchScalarGridSpec(num_sc...  64.2 us
    pallas_call x1, Pallas kernels, build(): pl.pallas_call(functools.partial(build_kernel, rows=128), grid_spec=pltpu...  56.5 us
    min x3, other arithmetic, shards(): clipped = jnp.clip(predicted - targets_all, -huber_cap, huber_cap)  5.12 us
  transfers between devices with their start and end apart: 3, of which 1 were waited for; matrix products, arithmetic and copies ran while one was open for 1% of the time, Pallas kernels for 0%

profile of v1, /device:TPU:0, one launch (start us, length us, event | category | flops | bytes accessed | tf_op | source)
XLA Modules:
  0.0 212.3 jit_solution(60925083407855436)
XLA Ops:
  0.6 0.6 collective-permute-start
  1.2 0.1 collective-permute-start.1
  1.3 1.9 collective-permute-done.1
  3.1 0.9 broadcast_select_fusion.5
  4.1 0.0 collective-permute-done
  4.1 1.1 broadcast_select_fusion.1
  5.2 0.8 fusion.fac_ref
  6.0 56.5 %build.1 = (bf16[2048,4096]{1,0:T(8,128)(2,1)}, bf16[2048,4096]{1,0:T(8,128)(2,1)}, f32[32,2048]{1,0:T(8,128)}) custom-call(s32[1]{0:T(128)} %bitcast.half_ref, bf16[2048,128]{1,0:T(8,128)(2,1)} %fusion.fac_ref, s32[128,8192]{1,0:T(8,128)} %freq_ref.1, s32[1,8192]{1,0:T(1,128)} %bitcast.10, f32[1,8192]{1,0:T(1,128)} %bitcast.6, f32[32,8192]{1,0:T(8,128)} %coef_ref.1), custom_call_target="tpu_custom_call" | custom-call | tf_op jit(solution)/shard_map/build/pallas_call | solution.py:90
  62.5 0.6 broadcast_in_dim.15.sq_ref
  63.1 20.1 %sum_over.4 = (f32[32,2048]{1,0:T(8,128)}, f32[8,128]{1,0:T(8,128)}) custom-call(f32[32,2048]{1,0:T(8,128)} %get-tuple-element.21.x_ref, f32[8,128]{1,0:T(8,128)} %broadcast_in_dim.15.sq_ref), custom_call_target="tpu_custom_call" | custom-call | tf_op jit(solution)/shard_map/sum_over/pallas_call | solution.py:272
  83.3 1.7 subtract_clamp_fusion.2.clip_ref
  84.9 21.3 %turn.3 = (f32[32,4096]{1,0:T(8,128)}, f32[32,2048]{1,0:T(8,128)}, f32[8,128]{1,0:T(8,128)}) custom-call(s32[1]{0:T(128)} %bitcast.half_ref, f32[32,2048]{1,0:T(8,128)} %subtract_clamp_fusion.2.clip_ref, f32[1,8192]{1,0:T(1,128)} %bitcast.7, bf16[2048,4096]{1,0:T(8,128)(2,1)} %get-tuple-element.23.hi_ref, bf16[2048,4096]{1,0:T(8,128)(2,1)} %get-tuple-element.24.lo_ref), custom_call_target="tpu_custom_call" | custom-call | tf_op jit(solution)/shard_map/turn/pallas_call | solution.py:144
  106.3 16.6 %sum_over.5 = (f32[32,2048]{1,0:T(8,128)}, f32[8,128]{1,0:T(8,128)}) custom-call(f32[32,2048]{1,0:T(8,128)} %get-tuple-element.26.x_ref, f32[8,128]{1,0:T(8,128)} %get-tuple-element.27.sq_ref), custom_call_target="tpu_custom_call" | custom-call | tf_op jit(solution)/shard_map/sum_over/pallas_call | solution.py:272
  122.9 1.2 slice.9
  124.8 0.0 copy-done
  124.8 1.7 subtract_clamp_fusion.1.clip_ref
  126.5 21.4 %turn.4 = (f32[32,4096]{1,0:T(8,128)}, f32[32,2048]{1,0:T(8,128)}, f32[8,128]{1,0:T(8,128)}) custom-call(s32[1]{0:T(128)} %bitcast.half_ref, f32[32,2048]{1,0:T(8,128)} %subtract_clamp_fusion.1.clip_ref, f32[1,8192]{1,0:T(1,128)} %bitcast.8, bf16[2048,4096]{1,0:T(8,128)(2,1)} %get-tuple-element.23.hi_ref, bf16[2048,4096]{1,0:T(8,128)(2,1)} %get-tuple-element.24.lo_ref), custom_call_target="tpu_custom_call" | custom-call | tf_op jit(solution)/shard_map/turn/pallas_call | solution.py:144
  147.8 16.4 %sum_over.6 = (f32[32,2048]{1,0:T(8,128)}, f32[8,128]{1,0:T(8,128)}) custom-call(f32[32,2048]{1,0:T(8,128)} %get-tuple-element.31.x_ref, f32[8,128]{1,0:T(8,128)} %get-tuple-element.32.sq_ref), custom_call_target="tpu_custom_call" | custom-call | tf_op jit(solution)/shard_map/sum_over/pallas_call | solution.py:272
  164.2 1.2 slice.10
  166.1 0.0 copy-done.2
  166.1 1.7 subtract_clamp_fusion
  167.9 21.5 %turn.5 = (f32[32,4096]{1,0:T(8,128)}, f32[32,2048]{1,0:T(8,128)}, f32[8,128]{1,0:T(8,128)}) custom-call(s32[1]{0:T(128)} %bitcast.half_ref, f32[32,2048]{1,0:T(8,128)} %get-tuple-element.40.clip_ref, f32[1,8192]{1,0:T(1,128)} %bitcast.9, bf16[2048,4096]{1,0:T(8,128)(2,1)} %get-tuple-element.23.hi_ref, bf16[2048,4096]{1,0:T(8,128)(2,1)} %get-tuple-element.24.lo_ref), custom_call_target="tpu_custom_call" | custom-call | tf_op jit(solution)/shard_map/turn/pallas_call | solution.py:144
  189.3 16.6 %sum_over.7 = (f32[32,2048]{1,0:T(8,128)}, f32[8,128]{1,0:T(8,128)}) custom-call(f32[32,2048]{1,0:T(8,128)} %get-tuple-element.36.x_ref, f32[8,128]{1,0:T(8,128)} %get-tuple-element.37.sq_ref), custom_call_target="tpu_custom_call" | custom-call | tf_op jit(solution)/shard_map/sum_over/pallas_call | solution.py:272
  205.9 1.2 slice.11
  207.8 0.0 copy-done.1
  207.8 0.0 copy-done.3
  207.9 1.3 multiply_subtract_fusion
  209.1 0.4 collective-permute-start.2
  209.6 1.6 dynamic-slice_subtract_fusion
  211.2 0.0 collective-permute-done.2
  211.2 0.1 broadcast_select_fusion.3
  211.2 1.0 pad_maximum_fusion
  (6 shorter events, 0.0 us)
Async XLA Ops:
  0.6 3.4 %collective-permute-start = (s32[1024,128]{1,0:T(8,128)}, s32[1024,128]{1,0:T(8,128)S(1)}, u32[]{:S(2)}, u32[]{:S(2)}) collective-permute-start(s32[1024,128]{1,0:T(8,128)} %param.6), channel_id=1, source_target_pairs={{0,8},{8,0},{1,9},{9,1},{2,10},{10,2},{3,11},{11,3},{4,12},{12,4},... | collective-permute-start | bytes 1572872 | tf_op jit(solution)/shard_map/ppermute | solution.py:295
  1.2 1.9 collective-permute-start.1
  84.9 39.8 %copy-start = (f32[32,2048]{1,0:T(8,128)S(1)}, f32[32,2048]{1,0:T(8,128)}, u32[]{:S(2)}) copy-start(f32[32,2048]{1,0:T(8,128)} %get-tuple-element.22) | copy-start | bytes 786436
  126.5 39.6 %copy-start.2 = (f32[32,2048]{1,0:T(8,128)S(1)}, f32[32,2048]{1,0:T(8,128)}, u32[]{:S(2)}) copy-start(f32[32,2048]{1,0:T(8,128)} %get-tuple-element.29) | copy-start | bytes 786436
  167.9 40.0 %copy-start.1 = (f32[32,8192]{1,0:T(8,128)S(1)}, f32[32,8192]{1,0:T(8,128)}, u32[]{:S(2)}) copy-start(f32[32,8192]{1,0:T(8,128)} %coef_ref.1) | copy-start | bytes 3145732
  167.9 40.0 %copy-start.3 = (f32[32,4096]{1,0:T(8,128)S(1)}, f32[32,4096]{1,0:T(8,128)}, u32[]{:S(2)}) copy-start(f32[32,4096]{1,0:T(8,128)} %get-tuple-element.25) | copy-start | bytes 1572868
  167.9 40.0 %copy-start.4 = (f32[32,4096]{1,0:T(8,128)S(1)}, f32[32,4096]{1,0:T(8,128)}, u32[]{:S(2)}) copy-start(f32[32,4096]{1,0:T(8,128)} %get-tuple-element.30) | copy-start | bytes 1572868
  209.1 2.0 collective-permute-start.2

commit v2 on v1

--- a/solution.py
+++ b/solution.py
@@ -63,6 +63,8 @@
     freq = freq_ref[...].astype(F32).astype(BF)
     phase = phase_ref[...].astype(F32) * (1.0 / 1024.0)
     chunks = fac_ref.shape[0] // rows
+    v = coef_ref.shape[0]
+    x = stacked(coef_ref[...] * amp_ref[...])
 
     def step(i, carry):
         at = pl.ds(pl.multiple_of(i * rows, rows), rows)
@@ -71,14 +73,12 @@
         hi, lo = split(c)
         hi_ref[at, :] = hi
         lo_ref[at, :] = lo
+        out = lax.dot_general(x, hi, NT, preferred_element_type=F32)
+        out = out + lax.dot_general(x, lo, NT, preferred_element_type=F32)
+        pred_ref[:, at] += out[:v] + out[v:]
         return carry
 
     lax.fori_loop(0, chunks, step, 0, unroll=2)
-    v = coef_ref.shape[0]
-    x = stacked(coef_ref[...] * amp_ref[...])
-    out = lax.dot_general(x, hi_ref[...], NT, preferred_element_type=F32)
-    out = out + lax.dot_general(x, lo_ref[...], NT, preferred_element_type=F32)
-    pred_ref[...] += out[:v] + out[v:]
 
 
 def build(half, factors, frequency, phases, amplitude, coeffs, tile):
@@ -88,7 +88,7 @@
     nb = mine // tile
     at = lambda i, h: (0, h[0] * nb + i)
     return pl.pallas_call(
-        functools.partial(build_kernel, rows=128),
+        functools.partial(build_kernel, rows=256),
         grid_spec=pltpu.PrefetchScalarGridSpec(
             num_scalar_prefetch=1,
             grid=(nb,),
@@ -171,9 +171,16 @@
 MESH = pl.DeviceIdType.MESH
 
 
-def sum_kernel(x_ref, sq_ref, out_ref, sqout_ref, from_pair, chip, pieces, result, sq_pair, sq_mine, sq_all, total,
-               pair_send, pair_recv, rs_send, rs_recv, ag_send, ag_recv, back_send, back_recv, sqp_sem, sqs_send, sqs_recv,
-               *, n, rows, width, per_row):
+def sum_kernel(*refs, n, rows, width, per_row, first, count):
+    if first:
+        x_ref, target_ref, pred_out, clip_out = refs[:4]
+        refs = refs[4:]
+    else:
+        x_ref, sq_ref, grad_ref, pred_ref, track_ref, target_ref, pred_out, track_out, clip_out, sq_out, grad_out = refs[:11]
+        grad_other, sq_pair, sq_mine, sq_all, sqp_sem, sqs_send, sqs_recv, grad_sem = refs[11:19]
+        refs = refs[19:]
+    from_pair, chip, pieces, result, total = refs[:5]
+    pair_send, pair_recv, rs_send, rs_recv, ag_send, ag_recv, back_send, back_recv = refs[5:]
     v, half_cols = chip.shape
     core = lax.axis_index("paths")
     me = lax.axis_index("feats")
@@ -197,8 +204,9 @@
         return pltpu.make_async_remote_copy(src, dst, ss, rs, device_id={"feats": j}, device_id_type=MESH)
 
     zero = 0
-    sq_copy = to_pair(sq_ref, sq_pair, sqp_sem.at[0], sqp_sem.at[1])
-    sq_copy.start()
+    if not first:
+        sq_copy = to_pair(sq_ref, sq_pair, sqp_sem.at[0], sqp_sem.at[1])
+        sq_copy.start()
     pair_copies = []
     for d in range(1, n + 1):
         j = lax.rem(me + d, n)
@@ -207,9 +215,12 @@
         pair_copies.append(to_pair(x_ref.at[r, c], from_pair.at[r2, c2], pair_send.at[d - 1], pair_recv.at[d - 1]))
         pair_copies[-1].start()
 
-    sq_copy.wait()
-    sq_mine[...] = sq_ref[...] + sq_pair[...]
-    sq_all[me] = sq_mine[...]
+    if not first:
+        grad_copy = to_pair(grad_ref, grad_other, grad_sem.at[0], grad_sem.at[1])
+        grad_copy.start()
+        sq_copy.wait()
+        sq_mine[...] = sq_ref[...] + sq_pair[...]
+        sq_all[me] = sq_mine[...]
     rs_copies, sq_copies = [], []
     for d in range(1, n + 1):
         j = lax.rem(me + d, n)
@@ -220,7 +231,7 @@
         if d < n:
             rs_copies.append(to_chip(chip.at[r2, c2], pieces.at[d - 1], rs_send.at[d - 1], rs_recv.at[d - 1], j))
             rs_copies[-1].start()
-    for d in range(1, n):
+    for d in range(1, 1 if first else n):
         j = lax.rem(me + d, n)
         sq_copies.append(to_chip(sq_mine, sq_all.at[me], sqs_send.at[d - 1], sqs_recv.at[d - 1], j))
         sq_copies[-1].start()
@@ -247,9 +258,11 @@
         r, c = spot(source, core * half_cols)
         back_copies.append(to_pair(result.at[r, c], result.at[r, c], back_send.at[d], back_recv.at[d]))
         back_copies[-1].start()
+    if not first:
+        grad_copy.wait()
+        grad_out[...] = grad_other[...]
     for copy in sq_copies:
         copy.wait()
-    sqout_ref[...] = jnp.broadcast_to(jnp.sum(jnp.sum(sq_all[...], axis=0), keepdims=True), sqout_ref.shape)
     for copy in pair_copies:
         copy.wait_send()
     for copy in rs_copies:
@@ -258,37 +271,92 @@
         copy.wait_send()
     for copy in back_copies:
         copy.wait()
-    out_ref[...] = result[...]
-
-
-def sum_over(partial, squares, n):
-    v, cols = partial.shape
+    if first:
+        predicted = result[...]
+    else:
+        squares = jnp.sum(sq_all[...], axis=0)
+        squares = jnp.sum(jnp.sum(squares, axis=0, keepdims=True), axis=1, keepdims=True)
+        scale = jnp.sqrt(squares / count + epsilon)
+        sq_out[...] = jnp.broadcast_to(scale, sq_out.shape)
+        tracked = momentum * track_ref[...] + result[...] / scale
+        track_out[...] = tracked
+        predicted = pred_ref[...] - step_rate * tracked
+    pred_out[...] = predicted
+    clip_out[...] = jnp.clip(predicted - target_ref[...], -huber_cap, huber_cap)
+
+
+def sum_over(operands, n, count):
+    v, cols = operands[0].shape
+    first = len(operands) == 2
     half_cols = cols // 2
     per_row = min(n, half_cols // 128)
     width = half_cols // per_row
     rows = v // (n // per_row)
     dma = pltpu.SemaphoreType.DMA
     vm = pl.BlockSpec(memory_space=pltpu.VMEM)
+    image = jax.ShapeDtypeStruct((v, cols), F32)
+    outs = [image, image]
+    extra = []
+    if not first:
+        grad = operands[2].shape
+        outs = [image, image, image, jax.ShapeDtypeStruct((8, 128), F32), jax.ShapeDtypeStruct(grad, F32)]
+        extra = [
+            pltpu.VMEM(grad, F32),
+            pltpu.VMEM((8, 128), F32),
+            pltpu.VMEM((8, 128), F32),
+            pltpu.VMEM((n, 8, 128), F32),
+            dma((2,)),
+            dma((n - 1,)),
+            dma((n - 1,)),
+            dma((2,)),
+        ]
     return pl.pallas_call(
-        functools.partial(sum_kernel, n=n, rows=rows, width=width, per_row=per_row),
-        in_specs=[vm, vm],
-        out_specs=[vm, vm],
-        out_shape=[jax.ShapeDtypeStruct((v, cols), F32), jax.ShapeDtypeStruct((8, 128), F32)],
-        scratch_shapes=[
+        functools.partial(sum_kernel, n=n, rows=rows, width=width, per_row=per_row, first=first, count=count),
+        in_specs=[vm] * len(operands),
+        out_specs=[vm] * len(outs),
+        out_shape=outs,
+        scratch_shapes=extra
+        + [
             pltpu.VMEM((v, half_cols), F32),
             pltpu.VMEM((v, half_cols), F32),
             pltpu.VMEM((n - 1, rows, width), F32),
             pltpu.VMEM((v, cols), F32),
-            pltpu.VMEM((8, 128), F32),
-            pltpu.VMEM((8, 128), F32),
-            pltpu.VMEM((n, 8, 128), F32),
             pltpu.VMEM((rows, width), F32),
-            dma((n,)), dma((n,)), dma((n - 1,)), dma((n - 1,)), dma((n - 1,)), dma((n - 1,)),
-            dma((n,)), dma((n,)), dma((2,)), dma((n - 1,)), dma((n - 1,)),
+            dma((n,)), dma((n,)), dma((n - 1,)), dma((n - 1,)), dma((n - 1,)), dma((n - 1,)), dma((n,)), dma((n,)),
         ],
-        compiler_params=pltpu.CompilerParams(collective_id=0, has_side_effects=True),
-        name="sum_over",
-    )(partial, squares)
+        compiler_params=pltpu.CompilerParams(collective_id=0 if first else 1, has_side_effects=True),
+        name="sum_first" if first else "sum_over",
+    )(*operands)
+
+
+def finish_kernel(*refs, iters):
+    init_ref, pred_ref = refs[:2]
+    mine, other, scales = refs[2 : 2 + iters], refs[2 + iters : 2 + 2 * iters], refs[2 + 2 * iters : 2 + 3 * iters]
+    coef_out, pred_out = refs[2 + 3 * iters :]
+    half = lax.axis_index("paths")
+    width = mine[0].shape[1]
+    own = pred_out.shape[1]
+    for grads, where in ((mine, half), (other, 1 - half)):
+        at = pl.ds(pl.multiple_of(where * width, width), width)
+        coeffs = init_ref[:, at]
+        velocity = jnp.zeros_like(coeffs)
+        for g, s in zip(grads, scales):
+            velocity = momentum * velocity + g[...] / s[0:1, 0:1]
+            coeffs = coeffs - step_rate * velocity
+        coef_out[:, at] = coeffs
+    pred_out[...] = pred_ref[:, pl.ds(pl.multiple_of(half * own, own), own)]
+
+
+def finish(init, predicted, mine, other, scales, own_paths):
+    v = init.shape[0]
+    vm = pl.BlockSpec(memory_space=pltpu.VMEM)
+    return pl.pallas_call(
+        functools.partial(finish_kernel, iters=len(mine)),
+        in_specs=[vm] * (2 + 3 * len(mine)),
+        out_specs=[vm, vm],
+        out_shape=[jax.ShapeDtypeStruct(init.shape, F32), jax.ShapeDtypeStruct((v, own_paths), F32)],
+        name="finish",
+    )(init, predicted, *mine, *other, *scales)
 
 
 def from_both(x, half, axis):
@@ -301,31 +369,24 @@
 def shards(total_features, chips, factors, frequency, phases, amplitude, targets, coeffs_init):
     half = lax.axis_index("paths")
     pick = half[None].astype(jnp.int32)
-    v, block = coeffs_init.shape
+    v = coeffs_init.shape[0]
     own_paths = targets.shape[1]
-    mine = block // 2
     factors_all = from_both(factors, half, 0).astype(F32).astype(BF)
     targets_all = from_both(targets, half, 1)
     amp_row = amplitude[None, :]
-    own_init = lax.dynamic_slice_in_dim(coeffs_init, half * mine, mine, 1)
 
     hi, lo, partial = build(pick, factors_all, frequency, phases[None, :], amp_row, coeffs_init, 256)
-    predicted, _ = sum_over(partial, jnp.zeros((8, 128), F32), chips)
-    coeffs = own_init
-    velocity = jnp.zeros_like(own_init)
+    predicted, clipped = sum_over((partial, targets_all), chips, None)
     tracked = jnp.zeros_like(predicted)
+    mine, other, scales = [], [], []
     for _ in range(ITERS):
-        clipped = jnp.clip(predicted - targets_all, -huber_cap, huber_cap)
         gradient, push, squares = turn(pick, clipped, amp_row, hi, lo, 512)
-        push, squares = sum_over(push, squares, chips)
-        squares = squares[0, 0]
-        scale = jnp.sqrt(squares / (v * total_features) + epsilon)
-        velocity = momentum * velocity + gradient / scale
-        coeffs = coeffs - step_rate * velocity
-        tracked = momentum * tracked + push / scale
-        predicted = predicted - step_rate * tracked
-    coeffs = from_both(coeffs, half, 1)
-    return coeffs, lax.dynamic_slice_in_dim(predicted, half * own_paths, own_paths, 1)
+        state = (push, squares, gradient, predicted, tracked, targets_all)
+        predicted, tracked, clipped, scale, partner = sum_over(state, chips, float(v * total_features))
+        mine.append(gradient)
+        other.append(partner)
+        scales.append(scale)
+    return finish(coeffs_init, predicted, mine, other, scales, own_paths)
 
 
 def solution(mesh):

time: 213 us -> 198 us (0.930)
  other arithmetic: 12 us -> 3.59 us
  local copies, waits for them, and re-layouts: 4.18 us -> 0.73 us
  between operations: 2.82 us -> 0.68 us
    min x3 -> x0, other arithmetic: 5.12 us -> none  [shards(): clipped = jnp.clip(predicted - targets_all, -huber_cap, huber_cap)]
    slice x3 -> x0, local copies, waits for them, and re-layouts: 3.57 us -> none  [shards(): squares = squares[0, 0]]
    sub x2 -> x0, other arithmetic: 2.87 us -> none  [the longest x1 1.59 us: shards(): predicted = predicted - step_rate * tracked]
    pallas_call x4, Pallas kernels: 69.7 us -> 72.2 us  [sum_over(): pl.pallas_call(functools.partial(sum_kernel, n=n, rows=rows, width=width,...]
    pallas_call x1 -> x2, Pallas kernels: 56.5 us -> 54.3 us  [the longest x1 50.2 us: build(): pl.pallas_call(functools.partial(build_kernel, rows=256), grid_spec=pltpu...]
  transfers between devices with their start and end apart: 3 -> 2, of which waited for: 1 -> 1; matrix products, arithmetic and copies ran while one was open for 1% -> 1% of each run, Pallas kernels for 0% -> 0%
where the time goes in v2:
time: 198 us; the launch traced here: 197 us
  Pallas kernels  190 us (96%)
  other arithmetic  3.59 us (2%)
    pallas_call x4, Pallas kernels, sum_over(): pl.pallas_call(functools.partial(sum_kernel, n=n, rows=rows, width=width,...  72.2 us
    pallas_call x3, Pallas kernels, turn(): pl.pallas_call(turn_kernel, grid_spec=pltpu.PrefetchScalarGridSpec(num_sc...  64 us
    pallas_call x1, Pallas kernels, build(): pl.pallas_call(functools.partial(build_kernel, rows=256), grid_spec=pltpu...  50.2 us
    pallas_call x1, Pallas kernels, finish(): pl.pallas_call(functools.partial(finish_kernel, iters=len(mine)), in_spec...  4.05 us
  transfers between devices with their start and end apart: 2, of which 1 were waited for; matrix products, arithmetic and copies ran while one was open for 1% of the time, Pallas kernels for 0%

profile of v2, /device:TPU:0, one launch (start us, length us, event | category | flops | bytes accessed | tf_op | source)
XLA Modules:
  0.0 197.2 jit_solution(9991560398780801575)
XLA Ops:
  0.6 0.6 collective-permute-start.1
  1.2 0.1 collective-permute-start
  1.3 1.1 collective-permute-done.1
  2.4 0.9 broadcast_select_fusion.3
  3.3 0.7 pad_maximum_fusion.refs_1_.refs_5_
  4.0 0.0 collective-permute-done
  4.0 1.1 broadcast_select_fusion.1
  5.1 0.8 fusion.fac_ref
  6.0 50.2 %build.1 = (bf16[2048,4096]{1,0:T(8,128)(2,1)}, bf16[2048,4096]{1,0:T(8,128)(2,1)}, f32[32,2048]{1,0:T(8,128)}) custom-call(s32[1]{0:T(128)} %bitcast.half_ref, bf16[2048,128]{1,0:T(8,128)(2,1)} %fusion.fac_ref, s32[128,8192]{1,0:T(8,128)} %freq_ref.1, s32[1,8192]{1,0:T(1,128)} %bitcast.7, f32[1,8192]{1,0:T(1,128)} %bitcast.3, f32[32,8192]{1,0:T(8,128)} %refs_0_.1), custom_call_target="tpu_custom_call" | custom-call | tf_op jit(solution)/shard_map/build/pallas_call | solution.py:90
  56.2 20.1 %sum_first.1 = (f32[32,2048]{1,0:T(8,128)}, f32[32,2048]{1,0:T(8,128)}) custom-call(f32[32,2048]{1,0:T(8,128)} %get-tuple-element.29.refs_0_, f32[32,2048]{1,0:T(8,128)} %pad_maximum_fusion.refs_1_.refs_5_), custom_call_target="tpu_custom_call" | custom-call | tf_op jit(solution)/shard_map/sum_first/pallas_call | solution.py:313
  76.3 21.3 %turn.3 = (f32[32,4096]{1,0:T(8,128)}, f32[32,2048]{1,0:T(8,128)}, f32[8,128]{1,0:T(8,128)}) custom-call(s32[1]{0:T(128)} %bitcast.half_ref, f32[32,2048]{1,0:T(8,128)} %get-tuple-element.30.clip_ref, f32[1,8192]{1,0:T(1,128)} %bitcast.4, bf16[2048,4096]{1,0:T(8,128)(2,1)} %get-tuple-element.31.hi_ref, bf16[2048,4096]{1,0:T(8,128)(2,1)} %get-tuple-element.32.lo_ref), custom_call_target="tpu_custom_call" | custom-call | tf_op jit(solution)/shard_map/turn/pallas_call | solution.py:144
  97.6 0.7 broadcast_in_dim.15.refs_4_
  98.4 17.3 %sum_over.3 = (f32[32,2048]{1,0:T(8,128)}, f32[32,2048]{1,0:T(8,128)}, f32[32,2048]{1,0:T(8,128)}, f32[8,128]{1,0:T(8,128)}, f32[32,4096]{1,0:T(8,128)}) custom-call(f32[32,2048]{1,0:T(8,128)} %get-tuple-element.33.refs_0_, f32[8,128]{1,0:T(8,128)} %get-tuple-element.34.refs_1_, f32[32,4096]{1,0:T(8,128)} %get-tuple-element.35.refs_2_, ...), custom_call_target="tpu_custom_call" | custom-call | tf_op jit(solution)/shard_map/sum_over/pallas_call | solution.py:313
  115.7 21.3 %turn.4 = (f32[32,4096]{1,0:T(8,128)}, f32[32,2048]{1,0:T(8,128)}, f32[8,128]{1,0:T(8,128)}) custom-call(s32[1]{0:T(128)} %bitcast.half_ref, f32[32,2048]{1,0:T(8,128)} %get-tuple-element.37.clip_ref, f32[1,8192]{1,0:T(1,128)} %bitcast.5, bf16[2048,4096]{1,0:T(8,128)(2,1)} %get-tuple-element.31.hi_ref, bf16[2048,4096]{1,0:T(8,128)(2,1)} %get-tuple-element.32.lo_ref), custom_call_target="tpu_custom_call" | custom-call | tf_op jit(solution)/shard_map/turn/pallas_call | solution.py:144
  137.0 17.4 %sum_over.4 = (f32[32,2048]{1,0:T(8,128)}, f32[32,2048]{1,0:T(8,128)}, f32[32,2048]{1,0:T(8,128)}, f32[8,128]{1,0:T(8,128)}, f32[32,4096]{1,0:T(8,128)}) custom-call(f32[32,2048]{1,0:T(8,128)} %get-tuple-element.38.refs_0_, f32[8,128]{1,0:T(8,128)} %get-tuple-element.39.refs_1_, f32[32,4096]{1,0:T(8,128)} %get-tuple-element.40.refs_2_.refs_3_, ...), custom_call_target="tpu_custom_call" | custom-call | tf_op jit(solution)/shard_map/sum_over/pallas_call | solution.py:313
  154.5 21.3 %turn.5 = (f32[32,4096]{1,0:T(8,128)}, f32[32,2048]{1,0:T(8,128)}, f32[8,128]{1,0:T(8,128)}) custom-call(s32[1]{0:T(128)} %bitcast.half_ref, f32[32,2048]{1,0:T(8,128)} %get-tuple-element.43.clip_ref, f32[1,8192]{1,0:T(1,128)} %bitcast.6, bf16[2048,4096]{1,0:T(8,128)(2,1)} %get-tuple-element.31.hi_ref, bf16[2048,4096]{1,0:T(8,128)(2,1)} %get-tuple-element.32.lo_ref), custom_call_target="tpu_custom_call" | custom-call | tf_op jit(solution)/shard_map/turn/pallas_call | solution.py:144
  175.8 17.3 %sum_over.5 = (f32[32,2048]{1,0:T(8,128)}, f32[32,2048]{1,0:T(8,128)}, f32[32,2048]{1,0:T(8,128)}, f32[8,128]{1,0:T(8,128)}, f32[32,4096]{1,0:T(8,128)}) custom-call(f32[32,2048]{1,0:T(8,128)} %get-tuple-element.44.refs_0_, f32[8,128]{1,0:T(8,128)} %get-tuple-element.45.refs_1_, f32[32,4096]{1,0:T(8,128)} %get-tuple-element.46.refs_2_.refs_4_, ...), custom_call_target="tpu_custom_call" | custom-call | tf_op jit(solution)/shard_map/sum_over/pallas_call | solution.py:313
  193.1 4.0 %finish.1 = (f32[32,8192]{1,0:T(8,128)}, f32[32,1024]{1,0:T(8,128)}) custom-call(f32[32,8192]{1,0:T(8,128)} %refs_0_.1, f32[32,2048]{1,0:T(8,128)} %get-tuple-element.49.refs_1_, f32[32,4096]{1,0:T(8,128)} %get-tuple-element.35.refs_2_, f32[32,4096]{1,0:T(8,128)} %get-tuple-element.40.refs_2_.refs_3_, f32[32,4096]{1,0:T(8,128)} %get-tuple-element.46.refs_2_.refs_4_, ...), custom_call_target="tpu_custom_call" | custom-call | tf_op jit(solution)/shard_map/finish/pallas_call | solution.py:353
Async XLA Ops:
  0.6 1.8 collective-permute-start.1
  1.2 2.8 %collective-permute-start = (s32[1024,128]{1,0:T(8,128)}, s32[1024,128]{1,0:T(8,128)S(1)}, u32[]{:S(2)}, u32[]{:S(2)}) collective-permute-start(s32[1024,128]{1,0:T(8,128)} %param.6), channel_id=1, source_target_pairs={{0,8},{8,0},{1,9},{9,1},{2,10},{10,2},{3,11},{11,3},{4,12},{12,4},... | collective-permute-start | bytes 1572872 | tf_op jit(solution)/shard_map/ppermute | solution.py:363
